TPU v7x, 32 devices: a whole 2x2x4 slice. The times are simulated.
32 devices in a mesh: grp: 4 (over x, core), col: 8 (over z, y).
Axes of the slice: x: 2, y: 2, z: 4, core: 2. Of those that a mesh axis runs over, the one named last changes fastest.
Arguments:
- diag_blocks: float32 [4096, 1024], P('grp', 'col'), may hold values from -8 to 48, as said below
- coupling: float32 [24576, 1024], P(('grp', 'col')), may hold values from -4 to 4
- parent_front: float32 [12288, 12288], P('grp', 'col'), may hold values from -6 to 6
- index_maps: int32 [4, 48], replicated, may hold values from 0 to 95, as said below
Outputs:
- assembled: float32 [12288, 12288], P('grp', 'col')
- diag_factor: float32 [4096, 1024], P('grp', 'col')
- panel: float32 [24576, 1024], P(('grp', 'col'))
Inputs may be any that keep to these rules, and one draw needn't show every extreme that they name: `diag_blocks`: each front's block of 1024 rows is symmetric positive definite. `index_maps`: the 48 entries of one row are distinct, and every parent block is named by some front.
All inputs are finite; a program needn't handle non-finite values.
Results may differ from a plain program's by a relative error of at most 0.0027.
Values may be sent and summed in bfloat16 or wider, within the bound.
No kernel may reach another device: no remote copies, remote signals or barrier semaphores. Data moves between devices by JAX's collectives and lax.ppermute only.
A program may use at most 192 MiB of HBM per device.

v0:
```python
import jax
import jax.numpy as jnp
from jax import lax
from jax.sharding import PartitionSpec as P

FRONTS = 4
BLK = 128
SBLK = 48
PBLK = 96


def swapped(block, axis, stride):
    count = lax.axis_size(axis)
    route = []
    for low in range(count):
        high = low | 1 << stride
        if high != low and high < count:
            route += [(low, high), (high, low)]
    return lax.ppermute(block, axis, route)


def place_rows(slab_blocks, source_block, present_count, count):
    picked = slab_blocks[jnp.arange(FRONTS)[:, None], source_block]
    picked = jnp.where(present_count[:, :, None, None] > 0, picked, jnp.zeros_like(picked))
    return jnp.transpose(picked, (1, 2, 0, 3)).reshape(count * BLK, -1)


def on_device(diag_blocks, coupling, parent_front, index_maps):
    groups = lax.axis_size("grp") // FRONTS
    swap_depth = groups.bit_length() - 1
    grp_index = lax.axis_index("grp")
    col_index = lax.axis_index("col")
    gathered = lax.all_gather(diag_blocks, "col", axis=1, tiled=True)
    for bit_pos in range(swap_depth):
        partner = swapped(gathered, "grp", bit_pos)
        is_upper = grp_index // 2**bit_pos % 2 == 1
        lower_half = jnp.where(is_upper, partner, gathered)
        upper_half = jnp.where(is_upper, gathered, partner)
        gathered = jnp.concatenate([lower_half, upper_half], axis=0)
    factor = jnp.linalg.cholesky(gathered)
    rows_here = diag_blocks.shape[0]
    col_width = diag_blocks.shape[1]
    local_start = grp_index % groups * rows_here
    factor_tile = lax.dynamic_slice(
        factor, (local_start, col_index * col_width), (rows_here, col_width)
    )
    panel_rows = lax.linalg.triangular_solve(
        factor, coupling, left_side=False, lower=True, transpose_a=True
    )
    panel_half = panel_rows.astype(jnp.bfloat16)
    panel_tiles = lax.all_to_all(panel_half, "col", split_axis=1, concat_axis=0, tiled=True)
    panel_slab = lax.all_gather(panel_tiles, "grp", axis=0, tiled=True)
    slab_blocks = panel_slab.reshape(FRONTS, SBLK, BLK, -1)
    parent_ids = jnp.arange(PBLK, dtype=jnp.int32)
    matches = (index_maps[:, :, None] == parent_ids[None, None, :]).astype(jnp.int32)
    present_count = jnp.sum(matches, axis=1)
    source_block = jnp.sum(matches * jnp.arange(SBLK, dtype=jnp.int32)[None, :, None], axis=1)
    row_count = parent_front.shape[0]
    contract = (((1,), (1,)), ((), ()))
    every_part = place_rows(slab_blocks, source_block, present_count, PBLK)
    col_operand = lax.all_to_all(every_part, "col", split_axis=0, concat_axis=1, tiled=True)
    row_part = lax.dynamic_slice_in_dim(every_part, grp_index * row_count, row_count, 0)
    update = lax.dot_general(
        lax.all_gather(row_part, "col", axis=1, tiled=True),
        col_operand,
        contract,
        preferred_element_type=jnp.float32,
    )
    merged = parent_front - update
    return (merged, factor_tile, panel_rows)


def solution(mesh):
    in_specs = (P("grp", "col"), P(("grp", "col"), None), P("grp", "col"), P())
    out_specs = (P("grp", "col"), P("grp", "col"), P(("grp", "col"), None))
    return jax.shard_map(
        on_device, mesh=mesh, in_specs=in_specs, out_specs=out_specs, check_vma=False
    )
```

profile of v0, /device:TPU:29, one launch (start us, length us, event | category | flops | bytes accessed | tf_op | source)
XLA Modules:
  0.0 1300.4 jit_solution(12328912837952660922)
XLA Ops:
  9.3 72.7 %all-gather.4.cloned.1.call-done = f32[1024,1024]{0,1:T(8,128)} async-done(((f32[1024,128]{0,1:T(8,128)}), f32[1024,1024]{0,1:T(8,128)}) %all-gather.4.cloned.1.call-update) | async-done | bytes 4194320 | tf_op jit(solution)/shard_map/all_gather | solution.py:33
  93.7 11.7 cholesky.223
  105.5 9.8 custom-call.62
  121.7 12.2 cholesky.244
  134.5 9.8 custom-call.63
  147.6 11.7 cholesky.468
  160.7 9.8 custom-call.64
  174.0 11.8 cholesky.487
  187.2 9.8 custom-call.65
  200.4 11.7 cholesky.506
  213.4 10.0 custom-call.66
  226.7 11.7 cholesky.526
  239.7 9.8 custom-call.67
  252.5 12.1 cholesky.546
  265.9 9.8 custom-call.68
  278.5 11.7 cholesky.564
  297.2 6.9 fusion.1
  304.1 29.0 %while.1 = (s32[]{:T(128)}, f32[1024,1024]{1,0:T(8,128)}, s32[8,2]{0,1:T(2,128)S(1)}, f32[8,128,128]{2,1,0:T(8,128)}, s32[]{:T(128)}) while((s32[]{:T(128)}, f32[1024,1024]{1,0:T(8,128)}, s32[8,2]{0,1:T(2,128)S(1)}, f32[8,128,128]{2,1,0:T(8,128)}, s32[]{:T(128)}) %tuple.72), condition=%wide.while_cond, body=%wide.while_body.sunk | while | flops 2 | bytes 132205 | solution.py:47
  333.2 80.2 %custom-call.69 = f32[8,128,128]{1,2,0:T(8,128)} custom-call(f32[8,128,128]{2,1,0:T(8,128)} %get-tuple-element.10), custom_call_target="InvertDiagBlocksLowerTriangular" | custom-call | tf_op jit(solution)/shard_map/triangular_solve | solution.py:47
  438.9 6.0 convolution_subtract_fusion.2
  445.4 40.0 %all_to_all.35 = bf16[768,8,128]{0,2,1:T(8,128)(2,1)S(1)} all-to-all(bf16[768,8,128]{0,2,1:T(8,128)(2,1)S(1)} %get-tuple-element.103), channel_id=1, replica_groups=mesh['grp'=4,'col'=8] {'col'}, dimensions={1} | all-to-all | bytes 3145728 | tf_op jit(solution)/shard_map/all_to_all | solution.py:51
  487.3 47.8 %all-gather.6.cloned.1.call-done = bf16[24576,128]{1,0:T(8,128)(2,1)} async-done(((bf16[6144,128]{1,0:T(8,128)(2,1)}), bf16[24576,128]{1,0:T(8,128)(2,1)}) %all-gather.6.cloned.1.call-update) | async-done | bytes 6291472 | tf_op jit(solution)/shard_map/all_gather | solution.py:52
  535.1 19.7 %gather_fusion = bf16[384,128,128]{2,1,0:T(8,128)(2,1)} fusion(bf16[4,48,128,128]{3,2,1,0:T(8,128)(2,1)} %bitcast.155, s32[384]{0:T(512)S(1)} %reshape.147), kind=kCustom, calls=%fused_computation | custom fusion | bytes 25168896 | tf_op jit(solution)/shard_map/gather | solution.py:23
  554.8 10.6 broadcast_select_fusion
  565.4 16.5 %copy.32 = bf16[96,128,4,128]{1,0,3,2:T(8,128)(2,1)} copy(bf16[96,128,4,128]{3,1,0,2:T(8,128)(2,1)} %broadcast_select_fusion) | data formatting | bytes 25165824 | tf_op jit(solution)/shard_map/jit(_where)/select_n | solution.py:24
  581.9 9.5 copy.38
  593.4 23.6 %all_to_all.29 = bf16[8,1536,512]{1,0,2:T(8,128)(2,1)} reshape(bf16[96,128,4,128]{1,0,3,2:T(8,128)(2,1)} %copy.32) | data formatting | bytes 25165824 | tf_op jit(solution)/shard_map/all_to_all | solution.py:61
  617.0 12.9 copy.34
  629.9 6.0 all-to-all-start.1
  640.3 377.6 %all-to-all-done.1 = bf16[8,1536,512]{1,2,0:T(8,128)(2,1)} async-done(((bf16[8,1536,512]{1,2,0:T(8,128)(2,1)}), bf16[8,1536,512]{1,2,0:T(8,128)(2,1)}, u32[]{:S(2)}, u32[]{:S(2)}) %all-to-all-start.1) | async-done | bytes 12582944 | tf_op jit(solution)/shard_map/all_to_all | solution.py:61
  1017.9 226.9 %all-gather.8.cloned.1.call-done = bf16[3072,4096]{0,1:T(8,128)(2,1)} async-done(((bf16[3072,512]{0,1:T(8,128)(2,1)}), bf16[3072,4096]{0,1:T(8,128)(2,1)}) %all-gather.8.cloned.1.call-update) | async-done | bytes 25165840 | tf_op jit(solution)/shard_map/all_gather | solution.py:64
  1244.8 48.9 %convolution_subtract_fusion = f32[3072,1536]{1,0:T(8,128)} fusion(f32[3072,1536]{1,0:T(8,128)} %param.6, bf16[3072,4096]{0,1:T(8,128)(2,1)} %all-gather.8.cloned.1.call-done, bf16[1536,4096]{0,1:T(8,128)(2,1)} %bitcast.40), kind=kOutput, calls=%fused_computation.3 | convolution fusion | flops 38659424256 | bytes 75497472 | tf_op jit(solution)/shard_map/dot_general | solution.py:63
  (115 shorter events, 111.6 us)
Async XLA Ops:
  7.2 74.9 %all-gather.4.cloned.1.call-start = ((), (), s32[]{:S(2)}) async-start(), calls=%async_computation.2 | async-start | bytes 4718592 | tf_op jit(solution)/shard_map/all_gather | solution.py:33
  9.3 525.9 %all-gather.6.cloned.1.call-start = ((), (), s32[]{:S(2)}) async-start(), calls=%async_computation.3 | async-start | bytes 7864320 | tf_op jit(solution)/shard_map/all_gather | solution.py:52
  91.8 1.9 copy-start
  297.2 116.2 %copy-start.3 = (f32[768,1024]{1,0:T(8,128)S(1)}, f32[768,1024]{1,0:T(8,128)}, u32[]{:S(2)}) copy-start(f32[768,1024]{1,0:T(8,128)} %param.5) | copy-start | bytes 9437188
  413.4 3.2 copy-start.4
  438.9 46.5 %copy-start.1 = (f32[768,1024]{0,1:T(8,128)}, f32[768,1024]{0,1:T(8,128)S(1)}, u32[]{:S(2)}) copy-start(f32[768,1024]{0,1:T(8,128)S(1)} %get-tuple-element.40) | copy-start | bytes 9437188
  485.4 1.6 copy-start.5
  487.0 757.7 %all-gather.8.cloned.1.call-start = ((), (), s32[]{:S(2)}) async-start(), calls=%async_computation.4 | async-start | bytes 28311552 | tf_op jit(solution)/shard_map/all_gather | solution.py:64
  629.9 6.0 copy-start.2
  629.9 387.9 %all-to-all-start.1 = ((bf16[8,1536,512]{1,2,0:T(8,128)(2,1)}), bf16[8,1536,512]{1,2,0:T(8,128)(2,1)}, u32[]{:S(2)}, u32[]{:S(2)}) async-start(bf16[8,1536,512]{1,2,0:T(8,128)(2,1)} %copy.34), calls=%async_computation.1 | async-start | bytes 25165824 | tf_op jit(solution)/shard_map/all_to_all | solution.py:61
Sparse Core Ops, SparseCore 0:
  10.7 71.3 all-gather.3
  487.1 47.9 all-gather.5
  593.5 651.2 all-gather.7
where the time goes:
time: 1310 us; the launch traced here: 1300 us
  waiting for transfers between devices  725 us (55%)
  other arithmetic  275 us (21%)
  local copies, waits for them, and re-layouts  132 us (10%)
  matrix products  103 us (8%)
  blocking collectives  40 us (3%)
  between operations  19.4 us (1%)
    all_to_all x1, waiting for transfers between devices, on_device(): lax.all_to_all(every_part, 'col', split_axis=0, concat_axis=1, tiled=True)  378 us
    all_gather x1, waiting for transfers between devices, on_device(): lax.all_gather(row_part, 'col', axis=1, tiled=True)  227 us
    another operation x30, other arithmetic, on_device(): factor = jnp.linalg.cholesky(gathered)  173 us
    another operation x3, other arithmetic, on_device(): lax.linalg.triangular_solve(factor, coupling, left_side=False, lower=True...  87.1 us
    all_gather x1, waiting for transfers between devices, on_device(): gathered = lax.all_gather(diag_blocks, 'col', axis=1, tiled=True)  72.7 us
    dot_general x1, matrix products, on_device(): lax.dot_general(lax.all_gather(row_part, 'col', axis=1, tiled=True), col_...  48.9 us
    all_gather x1, waiting for transfers between devices, on_device(): panel_slab = lax.all_gather(panel_tiles, 'grp', axis=0, tiled=True)  47.8 us
    all_to_all x1, blocking collectives, on_device(): lax.all_to_all(panel_half, 'col', split_axis=1, concat_axis=0, tiled=True)  40 us
  transfers between devices with their start and end apart: 4, of which 4 were waited for; matrix products, arithmetic and copies ran while one was open for 1% of the time, Pallas kernels for 0%

commit v1 on v0

--- a/solution.py
+++ b/solution.py
@@ -7,6 +7,29 @@
 BLK = 128
 SBLK = 48
 PBLK = 96
+
+
+def in_blocks(shard, dim, size):
+    dims = shard.shape
+    blocks = shard.reshape(*dims[:dim], size, dims[dim] // size, *dims[dim + 1 :])
+    return jnp.moveaxis(blocks, dim, 0)
+
+
+def joined_along(blocks, dim):
+    shape = list(blocks.shape[1:])
+    shape[dim] *= blocks.shape[0]
+    return jnp.moveaxis(blocks, 0, dim).reshape(shape)
+
+
+def sent_to_each(shard, axis, split_dim, concat_dim):
+    length, position = (lax.axis_size(axis), lax.axis_index(axis))
+    parts = in_blocks(shard, split_dim, length)
+    done = [parts[position]]
+    for step in range(1, length):
+        sent = parts[(position + step) % length]
+        done.append(lax.ppermute(sent, axis, [(i, (i + step) % length) for i in range(length)]))
+    parts = jnp.stack(done)[(position - jnp.arange(length)) % length]
+    return joined_along(parts, concat_dim)
 
 
 def swapped(block, axis, stride):
@@ -58,7 +81,7 @@
     row_count = parent_front.shape[0]
     contract = (((1,), (1,)), ((), ()))
     every_part = place_rows(slab_blocks, source_block, present_count, PBLK)
-    col_operand = lax.all_to_all(every_part, "col", split_axis=0, concat_axis=1, tiled=True)
+    col_operand = sent_to_each(every_part, "col", 0, 1)
     row_part = lax.dynamic_slice_in_dim(every_part, grp_index * row_count, row_count, 0)
     update = lax.dot_general(
         lax.all_gather(row_part, "col", axis=1, tiled=True),

time: 1310 us -> 1310 us (level)
  waiting for transfers between devices: 725 us -> 577 us
  local copies, waits for them, and re-layouts: 132 us -> 274 us
    all_to_all x1 -> x0, waiting for transfers between devices: 378 us -> none  [on_device(): lax.all_to_all(every_part, 'col', split_axis=0, concat_axis=1, tiled=True)]
    ppermute x0 -> x7, waiting for transfers between devices: none -> 371 us  [sent_to_each(): lax.ppermute(sent, axis, [(i, (i + step) % length) for i in range(length)])]
    all_gather x1, waiting for transfers between devices: 227 us -> 85.3 us  [on_device(): lax.all_gather(row_part, 'col', axis=1, tiled=True)]
    dynamic_slice x0 -> x8, local copies, waits for them, and re-layouts: none -> 99.2 us  [sent_to_each(): sent = parts[(position + step) % length]]
    all_to_all x2 -> x0, local copies, waits for them, and re-layouts: 36.5 us -> none  [on_device(): lax.all_to_all(every_part, 'col', split_axis=0, concat_axis=1, tiled=True)]
    unnamed x22 -> x32, local copies, waits for them, and re-layouts: 16.6 us -> 43.4 us
    another operation x24 -> x26, local copies, waits for them, and re-layouts: 29 us -> 53.9 us
    transpose x0 -> x1, local copies, waits for them, and re-layouts: none -> 16.7 us  [joined_along(): return jnp.moveaxis(blocks, 0, dim).reshape(shape)]
  transfers between devices with their start and end apart: 4 -> 10, of which waited for: 4 -> 6; matrix products, arithmetic and copies ran while one was open for 1% -> 14% of each run, Pallas kernels for 0% -> 0%
where the time goes in v1:
time: 1310 us; the launch traced here: 1290 us
  waiting for transfers between devices  577 us (44%)
  other arithmetic  275 us (21%)
  local copies, waits for them, and re-layouts  274 us (21%)
  matrix products  103 us (8%)
  blocking collectives  40 us (3%)
  between operations  19.5 us (1%)
    ppermute x7, waiting for transfers between devices, sent_to_each(): lax.ppermute(sent, axis, [(i, (i + step) % length) for i in range(length)])  371 us
    another operation x30, other arithmetic, on_device(): factor = jnp.linalg.cholesky(gathered)  173 us
    dynamic_slice x8, local copies, waits for them, and re-layouts, sent_to_each(): sent = parts[(position + step) % length]  99.2 us
    another operation x3, other arithmetic, on_device(): lax.linalg.triangular_solve(factor, coupling, left_side=False, lower=True...  87.1 us
    all_gather x1, waiting for transfers between devices, on_device(): lax.all_gather(row_part, 'col', axis=1, tiled=True)  85.3 us
    all_gather x1, waiting for transfers between devices, on_device(): gathered = lax.all_gather(diag_blocks, 'col', axis=1, tiled=True)  72.7 us
    dot_general x1, matrix products, on_device(): lax.dot_general(lax.all_gather(row_part, 'col', axis=1, tiled=True), col_...  48.9 us
    all_gather x1, waiting for transfers between devices, on_device(): panel_slab = lax.all_gather(panel_tiles, 'grp', axis=0, tiled=True)  47.8 us
  transfers between devices with their start and end apart: 10, of which 6 were waited for; matrix products, arithmetic and copies ran while one was open for 14% of the time, Pallas kernels for 0%

profile of v1, /device:TPU:29, one launch (start us, length us, event | category | flops | bytes accessed | tf_op | source)
XLA Modules:
  0.0 1293.7 jit_solution(10451000181351621414)
XLA Ops:
  9.3 72.7 %all-gather.4.cloned.1.call-done = f32[1024,1024]{0,1:T(8,128)} async-done(((f32[1024,128]{0,1:T(8,128)}), f32[1024,1024]{0,1:T(8,128)}) %all-gather.4.cloned.1.call-update) | async-done | bytes 4194320 | tf_op jit(solution)/shard_map/all_gather | solution.py:56
  93.7 11.7 cholesky.223
  105.5 9.8 custom-call.62
  121.7 12.2 cholesky.244
  134.5 9.8 custom-call.63
  147.6 11.7 cholesky.468
  160.7 9.8 custom-call.64
  174.0 11.8 cholesky.487
  187.2 9.8 custom-call.65
  200.4 11.7 cholesky.506
  213.4 10.0 custom-call.66
  226.7 11.7 cholesky.526
  239.7 9.8 custom-call.67
  252.5 12.1 cholesky.546
  265.9 9.8 custom-call.68
  278.5 11.7 cholesky.564
  304.1 29.0 %while.1 = (s32[]{:T(128)}, f32[1024,1024]{1,0:T(8,128)}, s32[8,2]{0,1:T(2,128)S(1)}, f32[8,128,128]{2,1,0:T(8,128)}, s32[]{:T(128)}) while((s32[]{:T(128)}, f32[1024,1024]{1,0:T(8,128)}, s32[8,2]{0,1:T(2,128)S(1)}, f32[8,128,128]{2,1,0:T(8,128)}, s32[]{:T(128)}) %tuple.78), condition=%wide.while_cond, body=%wide.while_body.sunk | while | flops 2 | bytes 132705 | solution.py:70
  333.2 80.2 %custom-call.69 = f32[8,128,128]{1,2,0:T(8,128)} custom-call(f32[8,128,128]{2,1,0:T(8,128)} %get-tuple-element.10), custom_call_target="InvertDiagBlocksLowerTriangular" | custom-call | tf_op jit(solution)/shard_map/triangular_solve | solution.py:70
  445.4 40.0 %all_to_all.16 = bf16[768,8,128]{0,2,1:T(8,128)(2,1)S(1)} all-to-all(bf16[768,8,128]{0,2,1:T(8,128)(2,1)S(1)} %get-tuple-element.108), channel_id=1, replica_groups=mesh['grp'=4,'col'=8] {'col'}, dimensions={1} | all-to-all | bytes 3145728 | tf_op jit(solution)/shard_map/all_to_all | solution.py:74
  487.3 47.8 %all-gather.6.cloned.1.call-done = bf16[24576,128]{1,0:T(8,128)(2,1)} async-done(((bf16[6144,128]{1,0:T(8,128)(2,1)}), bf16[24576,128]{1,0:T(8,128)(2,1)}) %all-gather.6.cloned.1.call-update) | async-done | bytes 6291472 | tf_op jit(solution)/shard_map/all_gather | solution.py:75
  535.1 19.7 %gather_fusion = bf16[384,128,128]{2,1,0:T(8,128)(2,1)} fusion(bf16[4,48,128,128]{3,2,1,0:T(8,128)(2,1)} %bitcast.178, s32[384]{0:T(512)S(1)} %reshape.196), kind=kCustom, calls=%fused_computation | custom fusion | bytes 25168896 | tf_op jit(solution)/shard_map/gather | solution.py:46
  554.8 10.6 broadcast_select_fusion
  565.4 16.5 %copy.33 = bf16[96,128,4,128]{1,0,3,2:T(8,128)(2,1)} copy(bf16[96,128,4,128]{3,1,0,2:T(8,128)(2,1)} %broadcast_select_fusion) | data formatting | bytes 25165824 | tf_op jit(solution)/shard_map/jit(_where)/select_n | solution.py:47
  593.5 23.6 %reshape_reshape.3 = bf16[8,1536,512]{1,0,2:T(8,128)(2,1)} reshape(bf16[96,128,4,128]{1,0,3,2:T(8,128)(2,1)} %copy.33) | data formatting | bytes 25165824 | tf_op jit(solution)/shard_map/reshape;reshape | solution.py:14
  617.1 44.1 %constant_dynamic-slice_fusion.2 = (bf16[1,1536,512]{1,0,2:T(2,128)(2,1)S(1)}, bf16[1,1536,512]{1,0,2:T(2,128)(2,1)}, bf16[1,1536,512]{1,0,2:T(2,128)(2,1)}, bf1...) fusion(bf16[8,1536,512]{1,0,2:T(8,128)(2,1)} %reshape_reshape.3, ...), kind=kLoop, calls=%fused_computation.165 | loop fusion | bytes 25165856 | tf_op jit(solution)/shard_map/dynamic_slice | solution.py:29
  738.6 68.6 %collective-permute-done = bf16[1536,512]{1,0:T(8,128)(2,1)} collective-permute-done((bf16[1536,512]{1,0:T(8,128)(2,1)}, bf16[1536,512]{1,0:T(8,128)(2,1)}, u32[]{:S(2)}, u32[]{:S(2)}) %collective-permute-start) | collective-permute-done | bytes 1572896 | tf_op jit(solution)/shard_map/ppermute | solution.py:30
  815.2 218.1 %collective-permute-done.3 = bf16[1536,512]{1,0:T(8,128)(2,1)} collective-permute-done((bf16[1536,512]{1,0:T(8,128)(2,1)}, bf16[1536,512]{1,0:T(8,128)(2,1)}, u32[]{:S(2)}, u32[]{:S(2)}) %collective-permute-start.3) | collective-permute-done | bytes 1572896 | tf_op jit(solution)/shard_map/ppermute | solution.py:30
  1035.9 84.0 %collective-permute-done.4 = bf16[1536,512]{1,0:T(8,128)(2,1)} collective-permute-done((bf16[1536,512]{1,0:T(8,128)(2,1)}, bf16[1536,512]{1,0:T(8,128)(2,1)}, u32[]{:S(2)}, u32[]{:S(2)}) %collective-permute-start.4) | collective-permute-done | bytes 1572896 | tf_op jit(solution)/shard_map/ppermute | solution.py:30
  1125.1 10.9 gather_fusion.1
  1136.0 16.7 %copy.43 = bf16[1536,8,512]{0,2,1:T(8,128)(2,1)} copy(bf16[1536,8,512]{2,0,1:T(8,128)(2,1)} %bitcast.177) | data formatting | bytes 25165824 | tf_op jit(solution)/shard_map/transpose | solution.py:21
  1152.7 85.3 %all-gather.8.cloned.1.call-done = bf16[3072,4096]{0,1:T(8,128)(2,1)} async-done(((bf16[3072,512]{0,1:T(8,128)(2,1)}), bf16[3072,4096]{0,1:T(8,128)(2,1)}) %all-gather.8.cloned.1.call-update) | async-done | bytes 25165840 | tf_op jit(solution)/shard_map/all_gather | solution.py:87
  1238.1 48.9 %convolution_subtract_fusion = f32[3072,1536]{1,0:T(8,128)} fusion(f32[3072,1536]{1,0:T(8,128)} %param.6, bf16[3072,4096]{0,1:T(8,128)(2,1)} %all-gather.8.cloned.1.call-done, bf16[1536,4096]{0,1:T(8,128)(2,1)} %bitcast.180), kind=kOutput, calls=%fused_computation.4 | convolution fusion | flops 38659424256 | bytes 75497472 | tf_op jit(solution)/shard_map/dot_general | solution.py:86
  (149 shorter events, 222.8 us)
Async XLA Ops:
  7.2 74.9 %all-gather.4.cloned.1.call-start = ((), (), s32[]{:S(2)}) async-start(), calls=%async_computation.1 | async-start | bytes 4718592 | tf_op jit(solution)/shard_map/all_gather | solution.py:56
  9.3 525.9 %all-gather.6.cloned.1.call-start = ((), (), s32[]{:S(2)}) async-start(), calls=%async_computation.2 | async-start | bytes 7864320 | tf_op jit(solution)/shard_map/all_gather | solution.py:75
  91.8 1.9 copy-start
  297.2 116.2 %copy-start.2 = (f32[768,1024]{1,0:T(8,128)S(1)}, f32[768,1024]{1,0:T(8,128)}, u32[]{:S(2)}) copy-start(f32[768,1024]{1,0:T(8,128)} %param.5) | copy-start | bytes 9437188
  413.4 3.2 copy-start.5
  438.9 46.5 %copy-start.1 = (f32[768,1024]{0,1:T(8,128)}, f32[768,1024]{0,1:T(8,128)S(1)}, u32[]{:S(2)}) copy-start(f32[768,1024]{0,1:T(8,128)S(1)} %get-tuple-element.45) | copy-start | bytes 9437188
  485.4 1.6 copy-start.6
  487.0 751.0 %all-gather.8.cloned.1.call-start = ((), (), s32[]{:S(2)}) async-start(), calls=%async_computation.3 | async-start | bytes 28311552 | tf_op jit(solution)/shard_map/all_gather | solution.py:87
  669.4 137.8 %collective-permute-start = (bf16[1536,512]{1,0:T(8,128)(2,1)}, bf16[1536,512]{1,0:T(8,128)(2,1)}, u32[]{:S(2)}, u32[]{:S(2)}) collective-permute-start(bf16[1536,512]{1,0:T(8,128)(2,1)} %bitcast.187), channel_id=1, source_target_pairs={{0,1},{1,2},{2,3},{3,4},{4,5},{5,6},{6,7},{7,0},{8,9},{9,10},{10,1... | collective-permute-start | bytes 4718600 | tf_op jit(solution)/shard_map/ppermute | solution.py:30
  677.7 132.1 %collective-permute-start.1 = (bf16[1536,512]{1,0:T(8,128)(2,1)}, bf16[1536,512]{1,0:T(8,128)(2,1)}, u32[]{:S(2)}, u32[]{:S(2)}) collective-permute-start(bf16[1536,512]{1,0:T(8,128)(2,1)} %bitcast.186), channel_id=1, source_target_pairs={{0,2},{1,3},{2,4},{3,5},{4,6},{5,7},{6,0},{7,1},{8,10},{9,11},{10,... | collective-permute-start | bytes 4718600 | tf_op jit(solution)/shard_map/ppermute | solution.py:30
  687.1 125.4 %collective-permute-start.2 = (bf16[1536,512]{1,0:T(8,128)(2,1)}, bf16[1536,512]{1,0:T(8,128)(2,1)}, u32[]{:S(2)}, u32[]{:S(2)}) collective-permute-start(bf16[1536,512]{1,0:T(8,128)(2,1)} %bitcast.188), channel_id=1, source_target_pairs={{0,3},{1,4},{2,5},{3,6},{4,7},{5,0},{6,1},{7,2},{8,11},{9,12},{10,... | collective-permute-start | bytes 4718600 | tf_op jit(solution)/shard_map/ppermute | solution.py:30
  711.0 322.3 %collective-permute-start.3 = (bf16[1536,512]{1,0:T(8,128)(2,1)}, bf16[1536,512]{1,0:T(8,128)(2,1)}, u32[]{:S(2)}, u32[]{:S(2)}) collective-permute-start(bf16[1536,512]{1,0:T(8,128)(2,1)} %bitcast.192), channel_id=1, source_target_pairs={{0,4},{1,5},{2,6},{3,7},{4,0},{5,1},{6,2},{7,3},{8,12},{9,13},{10,... | collective-permute-start | bytes 4718600 | tf_op jit(solution)/shard_map/ppermute | solution.py:30
  720.3 399.7 %collective-permute-start.4 = (bf16[1536,512]{1,0:T(8,128)(2,1)}, bf16[1536,512]{1,0:T(8,128)(2,1)}, u32[]{:S(2)}, u32[]{:S(2)}) collective-permute-start(bf16[1536,512]{1,0:T(8,128)(2,1)} %bitcast.191), channel_id=1, source_target_pairs={{0,5},{1,6},{2,7},{3,0},{4,1},{5,2},{6,3},{7,4},{8,13},{9,14},{10,... | collective-permute-start | bytes 4718600 | tf_op jit(solution)/shard_map/ppermute | solution.py:30
  735.7 71.4 %copy-start.4 = (bf16[1,1536,512]{2,1,0:T(8,128)(2,1)S(1)}, bf16[1,1536,512]{2,1,0:T(8,128)(2,1)}, u32[]{:S(2)}) copy-start(bf16[1,1536,512]{2,1,0:T(8,128)(2,1)} %copy.41) | copy-start | bytes 4718596
  735.7 74.1 %copy-start.3 = (bf16[1,1536,512]{2,1,0:T(8,128)(2,1)S(1)}, bf16[1,1536,512]{2,1,0:T(8,128)(2,1)}, u32[]{:S(2)}) copy-start(bf16[1,1536,512]{2,1,0:T(8,128)(2,1)} %copy.42) | copy-start | bytes 4718596
  807.2 315.4 %collective-permute-start.5 = (bf16[1536,512]{1,0:T(8,128)(2,1)S(1)}, bf16[1536,512]{1,0:T(8,128)(2,1)S(1)}, u32[]{:S(2)}, u32[]{:S(2)}) collective-permute-start(bf16[1536,512]{1,0:T(8,128)(2,1)S(1)} %bitcast.190), channel_id=1, source_target_pairs={{0,6},{1,7},{2,0},{3,1},{4,2},{5,3},{6,4},{7,5},{8,14},{9,15},{10,... | collective-permute-start | bytes 4718600 | tf_op jit(solution)/shard_map/ppermute | solution.py:30
  809.8 314.0 %collective-permute-start.6 = (bf16[1536,512]{1,0:T(8,128)(2,1)S(1)}, bf16[1536,512]{1,0:T(8,128)(2,1)S(1)}, u32[]{:S(2)}, u32[]{:S(2)}) collective-permute-start(bf16[1536,512]{1,0:T(8,128)(2,1)S(1)} %bitcast.189), channel_id=1, source_target_pairs={{0,7},{1,0},{2,1},{3,2},{4,3},{5,4},{6,5},{7,6},{8,15},{9,8},{10,9... | collective-permute-start | bytes 4718600 | tf_op jit(solution)/shard_map/ppermute | solution.py:30
Sparse Core Ops, SparseCore 0:
  10.7 71.3 all-gather.3
  487.1 47.9 all-gather.5
  593.5 644.5 all-gather.7
